TPU v7x, 256 devices: a whole 4x4x8 slice. The times are simulated.
256 devices in a mesh: wedge: 4 (over y), box: 64 (over x, z, core).
Axes of the slice: x: 4, y: 4, z: 8, core: 2. Of those that a mesh axis runs over, the one named last changes fastest.
Arguments:
- densities: bfloat16 [2048, 4, 128], P('box', 'wedge'), may hold values from -6 to 6
- up_ops: bfloat16 [96, 128, 128], replicated, may hold values from -0.5 to 0.5
- trans_ops: bfloat16 [16, 128, 128], replicated, may hold values from -0.125 to 0.125
- down_ops: bfloat16 [96, 128, 128], replicated, may hold values from -0.0546875 to 0.0546875
- read_table: int32 [64, 128], P('box'), may hold values from 0 to 2047, as said below
- interaction: int32 [2048, 96, 16], P('box', 'wedge'), may hold values from 0 to 127
Outputs:
- potentials: bfloat16 [2048, 4, 128], P('box', 'wedge')
Inputs may be any that keep to these rules, and one draw needn't show every extreme that they name: `read_table`: row r holds, for each box group o in order, 2 distinct boxes owned by box group o, numbered o * 32 to o * 32 + 31. interaction[b, w, k] indexes row b // 32 of read_table.
All inputs are finite; a program needn't handle non-finite values.
Results may differ from a plain program's by a relative error of at most 0.0057.
Values may be sent and summed in bfloat16 or wider, within the bound.
No kernel may reach another device: no remote copies, remote signals or barrier semaphores. Data moves between devices by JAX's collectives and lax.ppermute only.
A program may use at most 128 MiB of HBM per device.

v0:
```python
import jax
import jax.numpy as jnp
from jax import lax
from jax.sharding import PartitionSpec as P


def body(densities, up_ops, trans_ops, down_ops, read_table, interaction):
    boxes_here = densities.shape[0]
    fields_here = densities.shape[1]
    wedge_count = up_ops.shape[0]
    coeffs = up_ops.shape[1]
    wedge_groups = lax.axis_size("wedge")
    box_groups = lax.axis_size("box")
    wedge_here = wedge_count // wedge_groups
    fields = fields_here * wedge_groups
    read_count = read_table.shape[1]
    per_owner = read_count // box_groups
    first_box = lax.axis_index("box") * boxes_here
    wanted = lax.all_to_all(
        read_table.reshape(box_groups, per_owner), "box", split_axis=0, concat_axis=0, tiled=True
    )
    local_ids = wanted - first_box
    by_field = jnp.einsum(
        "bfp,wcp->bwfc", densities, up_ops, preferred_element_type=jnp.float32
    ).astype(jnp.bfloat16)
    equivalents = lax.all_to_all(by_field, "wedge", split_axis=1, concat_axis=2, tiled=True)
    picked = equivalents[local_ids]
    fetched = lax.all_to_all(picked, "box", split_axis=0, concat_axis=0, tiled=True)
    fetched = fetched.reshape(read_count, wedge_here, fields, coeffs)
    fetched_flat = fetched.reshape(read_count, wedge_here, fields * coeffs)
    list_len = interaction.shape[2]
    by_wedge = interaction.transpose(1, 0, 2).reshape(wedge_here, boxes_here * list_len)
    slot_ids = jnp.arange(read_count, dtype=jnp.int32)
    selector = (by_wedge[:, :, None] == slot_ids[None, None, :]).astype(jnp.bfloat16)
    sources = jnp.einsum(
        "wnr,rwx->wnx", selector, fetched_flat, preferred_element_type=jnp.float32
    ).astype(jnp.bfloat16)
    sources = sources.reshape(wedge_here, boxes_here, list_len, fields, coeffs)
    local_coeffs = jnp.einsum(
        "wbkfc,kdc->wbfd", sources, trans_ops, preferred_element_type=jnp.float32
    ).astype(jnp.bfloat16)
    arrived_back = lax.all_to_all(local_coeffs, "wedge", split_axis=2, concat_axis=0, tiled=True)
    potentials = jnp.einsum(
        "wbfc,wpc->bfp", arrived_back, down_ops, preferred_element_type=jnp.float32
    )
    return potentials.astype(jnp.bfloat16)


def solution(mesh):
    in_specs = (P("box", "wedge", None), P(), P(), P(), P("box", None), P("box", "wedge", None))
    out_specs = P("box", "wedge", None)
    return jax.shard_map(body, mesh=mesh, in_specs=in_specs, out_specs=out_specs, check_vma=False)
```

profile of v0, /device:TPU:1, one launch (start us, length us, event | category | flops | bytes accessed | tf_op | source)
XLA Modules:
  0.0 199.6 jit_solution(14767120359650167623)
XLA Ops:
  0.0 0.0 copy-start
  0.0 0.5 broadcast.30
  0.5 1.6 reduce.3
  2.1 0.8 all_to_all.37
  2.8 13.0 %all-to-all-start.1 = ((s32[64,1,2]{2,1,0:T(1,128)}), s32[64,1,2]{2,1,0:T(1,128)S(1)}, u32[]{:S(2)}, u32[]{:S(2)}) async-start(s32[64,1,2]{2,1,0:T(1,128)} %bitcast.9), calls=%async_computation.1 | async-start | bytes 65536 | tf_op jit(solution)/shard_map/all_to_all | solution.py:19
  15.8 0.0 copy-done
  15.8 2.8 %fusion.5 = bf16[32,96,1,128]{3,0,2,1:T(8,128)(2,1)} fusion(bf16[96,128,128]{2,1,0:T(8,128)(2,1)S(1)} %copy-done, bf16[32,1,128]{2,0,1:T(8,128)(2,1)} %param.6), kind=kOutput, calls=%fused_computation.8 | convolution fusion | flops 101056512 | bytes 3940352 | tf_op jit(solution)/shard_map/bfp,wcp->bwfc/dot_general | solution.py:23
  18.6 6.5 %all-to-all-done.1 = s32[64,1,2]{2,1,0:T(1,128)S(1)} async-done(((s32[64,1,2]{2,1,0:T(1,128)}), s32[64,1,2]{2,1,0:T(1,128)S(1)}, u32[]{:S(2)}, u32[]{:S(2)}) %all-to-all-start.1) | async-done | bytes 544 | tf_op jit(solution)/shard_map/all_to_all | solution.py:19
  25.1 4.2 %all-to-all-start = ((bf16[32,96,1,128]{3,0,2,1:T(8,128)(2,1)}), bf16[32,96,1,128]{3,0,2,1:T(8,128)(2,1)}, u32[]{:S(2)}, u32[]{:S(2)}) async-start(bf16[32,96,1,128]{3,0,2,1:T(8,128)(2,1)} %fusion.5), calls=%async_computation | async-start | bytes 1572864 | tf_op jit(solution)/shard_map/all_to_all | solution.py:26
  29.3 0.1 copy.32
  29.4 0.1 copy.33
  29.5 0.1 reshape.45
  29.7 11.2 %all-to-all-done = bf16[32,96,1,128]{3,0,2,1:T(8,128)(2,1)} async-done(((bf16[32,96,1,128]{3,0,2,1:T(8,128)(2,1)}), bf16[32,96,1,128]{3,0,2,1:T(8,128)(2,1)}, u32[]{:S(2)}, u32[]{:S(2)}) %all-to-all-start) | async-done | bytes 786464 | tf_op jit(solution)/shard_map/all_to_all | solution.py:26
  40.9 2.3 %copy.30 = bf16[32,96,1,128]{3,1,0,2:T(8,128)(2,1)} copy(bf16[32,96,1,128]{3,0,2,1:T(8,128)(2,1)} %all-to-all-done) | data formatting | bytes 1572864 | tf_op jit(solution)/shard_map/all_to_all | solution.py:26
  43.2 3.7 %gather_fusion = bf16[128,24,4,128]{3,1,2,0:T(8,128)(2,1)} fusion(bf16[32,24,4,128]{3,1,2,0:T(8,128)(2,1)} %bitcast.49, s32[1024]{0:T(1024)S(1)} %pad_clamp_fusion), kind=kCustom, calls=%fused_computation | custom fusion | bytes 6291968 | tf_op jit(solution)/shard_map/gather | solution.py:27
  46.9 5.2 %copy.34 = bf16[64,2,24,4,128]{4,3,1,2,0:T(4,128)(2,1)} copy(bf16[64,2,24,4,128]{4,2,3,1,0:T(8,128)(2,1)} %bitcast.50) | data formatting | bytes 6291456 | tf_op jit(solution)/shard_map/gather | solution.py:27
  52.1 6.8 %all-to-all-start.2 = ((bf16[64,2,24,4,128]{4,3,1,2,0:T(4,128)(2,1)}), bf16[64,2,24,4,128]{4,3,1,2,0:T(4,128)(2,1)}, u32[]{:S(2)}, u32[]{:S(2)}) async-start(bf16[64,2,24,4,128]{4,3,1,2,0:T(4,128)(2,1)} %copy.34), calls=%async_computation.2 | async-start | bytes 6291456 | tf_op jit(solution)/shard_map/all_to_all | solution.py:28
  58.9 1.1 copy.28
  60.0 0.8 eq.15
  60.8 71.5 %all-to-all-done.2 = bf16[64,2,24,4,128]{4,3,1,2,0:T(4,128)(2,1)} async-done(((bf16[64,2,24,4,128]{4,3,1,2,0:T(4,128)(2,1)}), bf16[64,2,24,4,128]{4,3,1,2,0:T(4,128)(2,1)}, u32[]{:S(2)}, u32[]{:S(2)}) %all-to-all-start.2) | async-done | bytes 3145760 | tf_op jit(solution)/shard_map/all_to_all | solution.py:28
  132.3 5.2 %copy.35 = bf16[64,2,24,4,128]{4,3,1,0,2:T(4,128)(2,1)} copy(bf16[64,2,24,4,128]{4,3,1,2,0:T(4,128)(2,1)} %all-to-all-done.2) | data formatting | bytes 6291456 | tf_op jit(solution)/shard_map/all_to_all | solution.py:28
  137.5 0.0 copy-start.2
  137.5 5.7 %reshape_reshape.3 = bf16[128,24,512]{2,0,1:T(8,128)(2,1)} reshape(bf16[64,2,24,4,128]{4,3,1,0,2:T(4,128)(2,1)} %copy.35) | data formatting | bytes 6291456 | tf_op jit(solution)/shard_map/reshape;reshape | solution.py:30
  143.3 0.0 copy-done.2
  143.3 8.3 %convolution_convert_fusion = bf16[24,512,512]{2,1,0:T(8,128)(2,1)} fusion(bf16[128,24,512]{2,0,1:T(8,128)(2,1)} %reshape_reshape.3, s32[24,512]{1,0:T(8,128)S(1)} %copy-done.2), kind=kOutput, calls=%fused_computation.3 | convolution fusion | flops 1618477056 | bytes 15777792 | tf_op jit(solution)/shard_map/wnr,rwx->wnx/dot_general | solution.py:35
  151.6 18.2 %reshape.41 = bf16[24,32,16,4,128]{4,3,2,1,0:T(4,128)(2,1)} reshape(bf16[24,512,512]{2,1,0:T(8,128)(2,1)} %convolution_convert_fusion) | data formatting | bytes 25165824 | tf_op jit(solution)/shard_map/reshape | solution.py:38
  169.8 13.2 %bitcast_convert_fusion = bf16[24,32,4,128]{3,1,2,0:T(8,128)(2,1)S(1)} fusion(bf16[24,32,16,4,128]{4,3,2,1,0:T(4,128)(2,1)} %reshape.41, bf16[16,128,128]{2,1,0:T(8,128)(2,1)} %param.8), kind=kOutput, calls=%fused_computation.6 | convolution fusion | flops 1611005952 | bytes 13893632 | tf_op jit(solution)/shard_map/wbkfc,kdc->wbfd/dot_general | solution.py:39
  182.9 0.0 copy-start.1
  182.9 0.1 copy.37
  183.0 14.9 %all_to_all.47 = bf16[24,32,4,128]{3,1,0,2:T(8,128)(2,1)S(1)} all-to-all(bf16[24,32,4,128]{3,1,0,2:T(8,128)(2,1)S(1)} %copy.37), channel_id=1, replica_groups=mesh['wedge'=4,'box'=64] {'wedge'}, dimensions={2} | all-to-all | bytes 1572864 | tf_op jit(solution)/shard_map/all_to_all | solution.py:42
  197.9 0.0 copy-done.1
  197.9 1.7 fusion.7
  (2 shorter events, 0.0 us)
Async XLA Ops:
  0.0 15.8 %copy-start = (bf16[96,128,128]{2,1,0:T(8,128)(2,1)S(1)}, bf16[96,128,128]{2,1,0:T(8,128)(2,1)}, u32[]{:S(2)}) copy-start(bf16[96,128,128]{2,1,0:T(8,128)(2,1)} %param.7) | copy-start | bytes 9437188
  2.8 22.3 %all-to-all-start.1 = ((s32[64,1,2]{2,1,0:T(1,128)}), s32[64,1,2]{2,1,0:T(1,128)S(1)}, u32[]{:S(2)}, u32[]{:S(2)}) async-start(s32[64,1,2]{2,1,0:T(1,128)} %bitcast.9), calls=%async_computation.1 | async-start | bytes 65536 | tf_op jit(solution)/shard_map/all_to_all | solution.py:19
  25.1 15.7 %all-to-all-start = ((bf16[32,96,1,128]{3,0,2,1:T(8,128)(2,1)}), bf16[32,96,1,128]{3,0,2,1:T(8,128)(2,1)}, u32[]{:S(2)}, u32[]{:S(2)}) async-start(bf16[32,96,1,128]{3,0,2,1:T(8,128)(2,1)} %fusion.5), calls=%async_computation | async-start | bytes 1572864 | tf_op jit(solution)/shard_map/all_to_all | solution.py:26
  52.1 80.2 %all-to-all-start.2 = ((bf16[64,2,24,4,128]{4,3,1,2,0:T(4,128)(2,1)}), bf16[64,2,24,4,128]{4,3,1,2,0:T(4,128)(2,1)}, u32[]{:S(2)}, u32[]{:S(2)}) async-start(bf16[64,2,24,4,128]{4,3,1,2,0:T(4,128)(2,1)} %copy.34), calls=%async_computation.2 | async-start | bytes 6291456 | tf_op jit(solution)/shard_map/all_to_all | solution.py:28
  137.5 5.7 %copy-start.2 = (s32[24,512]{1,0:T(8,128)S(1)}, s32[24,512]{1,0:T(8,128)}, u32[]{:S(2)}) copy-start(s32[24,512]{1,0:T(8,128)} %eq.15) | copy-start | bytes 147460
  182.9 14.9 %copy-start.1 = (bf16[96,128,128]{2,1,0:T(8,128)(2,1)S(1)}, bf16[96,128,128]{2,1,0:T(8,128)(2,1)}, u32[]{:S(2)}) copy-start(bf16[96,128,128]{2,1,0:T(8,128)(2,1)} %param.9) | copy-start | bytes 9437188
where the time goes:
time: 201 us; the launch traced here: 200 us
  waiting for transfers between devices  89.2 us (44%)
  local copies, waits for them, and re-layouts  43.9 us (22%)
  matrix products  26 us (13%)
  starting transfers between devices  23.9 us (12%)
  blocking collectives  14.9 us (7%)
    all_to_all x1, waiting for transfers between devices, body(): lax.all_to_all(picked, 'box', split_axis=0, concat_axis=0, tiled=True)  71.5 us
    reshape x1, local copies, waits for them, and re-layouts, body(): sources = sources.reshape(wedge_here, boxes_here, list_len, fields, coeffs)  18.2 us
    all_to_all x1, blocking collectives, body(): lax.all_to_all(local_coeffs, 'wedge', split_axis=2, concat_axis=0, tiled=...  14.9 us
    dot_general x1, matrix products, body(): jnp.einsum('wbkfc,kdc->wbfd', sources, trans_ops, preferred_element_type=...  13.2 us
    all_to_all x1, starting transfers between devices, body(): lax.all_to_all(read_table.reshape(box_groups, per_owner), 'box', split_ax...  13 us
    all_to_all x1, waiting for transfers between devices, body(): lax.all_to_all(by_field, 'wedge', split_axis=1, concat_axis=2, tiled=True)  11.2 us
    gather x2, local copies, waits for them, and re-layouts, body(): picked = equivalents[local_ids]  8.94 us
    dot_general x1, matrix products, body(): jnp.einsum('wnr,rwx->wnx', selector, fetched_flat, preferred_element_type...  8.33 us
  transfers between devices with their start and end apart: 3, of which 3 were waited for; matrix products, arithmetic and copies ran while one was open for 3% of the time, Pallas kernels for 0%

commit v1 on v0

v1 whole, which is shorter than its diff:
```python
import jax
import jax.numpy as jnp
from jax import lax
from jax.experimental import pallas as pl
from jax.experimental.pallas import tpu as pltpu
from jax.sharding import PartitionSpec as P

BF = jnp.bfloat16
F32 = jnp.float32
NT = (((1,), (1,)), ((), ()))
GROUP = 8


def columns_kernel(list_ref, out_ref):
    wedges, length, boxes = list_ref.shape
    flat = list_ref[...].astype(F32).reshape(wedges * length, boxes)
    out_ref[...] = flat.T.astype(BF)


def selector_kernel(columns_ref, target_ref, trans_ref, sel_ref, pick_ref, tcat_ref):
    step = pl.program_id(0)
    slots = target_ref.shape[1]
    boxes = columns_ref.shape[1]
    length = trans_ref.shape[0]
    group = sel_ref.shape[0]
    lane = lax.broadcasted_iota(jnp.int32, (boxes, slots), 1).astype(F32).astype(BF)
    cols = columns_ref[0]
    for w in range(group):
        for k in range(length):
            at = w * length + k
            hit = jnp.broadcast_to(cols[:, at : at + 1], (boxes, slots)) == lane
            sel_ref[w, (k // 2) * boxes : (k // 2 + 1) * boxes, (k % 2) * slots : (k % 2 + 1) * slots] = (
                jnp.where(hit, jnp.ones_like(lane), jnp.zeros_like(lane))
            )

    @pl.when(step == 0)
    def _():
        total = pick_ref.shape[1]
        wide = jnp.broadcast_to(target_ref[...].astype(F32), (slots, slots)).T
        for j in range(total // slots):
            number = lax.broadcasted_iota(jnp.int32, (slots, slots), 1).astype(F32) + float(j * slots)
            pick_ref[:, j * slots : (j + 1) * slots] = jnp.where(wide == number, 1.0, 0.0).astype(BF)
        c = trans_ref.shape[2]
        for k in range(length):
            tcat_ref[k * c : (k + 1) * c, :] = trans_ref[k].T


def main_kernel(near_ref, far_ref, pick_ref, sel_ref, up_ref, tcat_ref, down_ref, out_ref, dens, blocks, wide, acc):
    step = pl.program_id(0)
    group, c, p = up_ref.shape
    half = near_ref.shape[0]
    slots = pick_ref.shape[0]
    boxes = out_ref.shape[0]
    pairs = sel_ref.shape[1] // boxes

    @pl.when(step == 0)
    def _():
        picked = jnp.dot(pick_ref[:, :half], near_ref[...], preferred_element_type=F32)
        picked += jnp.dot(pick_ref[:, half:], far_ref[...], preferred_element_type=F32)
        dens[...] = picked.astype(BF)
        blocks[...] = jnp.zeros_like(blocks)
        acc[...] = jnp.zeros_like(acc)

    equivalents = lax.dot_general(
        dens[...], up_ref[...].reshape(group * c, p), NT, preferred_element_type=F32
    ).astype(BF)
    for w in range(group):
        one = equivalents[:, w * c : (w + 1) * c]
        blocks[w, :slots, :c] = one
        blocks[w, slots:, c:] = one
    for w in range(group):
        sources = jnp.dot(sel_ref[w], blocks[w], preferred_element_type=F32).astype(BF)
        for j in range(pairs):
            wide[w * boxes : (w + 1) * boxes, j * 2 * c : (j + 1) * 2 * c] = sources[j * boxes : (j + 1) * boxes]
    local = jnp.dot(wide[...], tcat_ref[...], preferred_element_type=F32).astype(BF)
    total = acc[...]
    for w in range(group):
        total += lax.dot_general(
            local[w * boxes : (w + 1) * boxes], down_ref[w], NT, preferred_element_type=F32
        )
    acc[...] = total

    @pl.when(step == pl.num_programs(0) - 1)
    def _():
        out_ref[...] = total.astype(BF)


def solution(mesh):
    x_chips, z_chips, cores = 4, 8, 2
    groups = [[(x * z_chips + z) * cores + c for x in range(x_chips) for z in range(z_chips)] for c in range(cores)]
    swap = [(i, i ^ 1) for i in range(x_chips * z_chips * cores)]

    def body(densities, up_ops, trans_ops, down_ops, read_table, interaction):
        boxes, _, p = densities.shape
        wedges, c, _ = up_ops.shape
        wedge_here, length = interaction.shape[1:]
        wedge_groups = wedges // wedge_here
        slots = read_table.shape[1]
        chips = len(groups[0])
        half = chips * boxes

        own = densities.reshape(boxes, p)
        copies = jnp.broadcast_to(own[None], (chips, boxes, p))
        near = lax.all_to_all(copies, "box", 0, 0, axis_index_groups=groups).reshape(half, p)

        lists = interaction.transpose(1, 2, 0)
        columns = pl.pallas_call(
            columns_kernel,
            out_shape=jax.ShapeDtypeStruct((boxes, wedge_here * length), BF),
            name="columns",
        )(lists)
        spread = jnp.broadcast_to(columns[None], (wedge_groups,) + columns.shape)
        spread = lax.all_to_all(spread, "wedge", 0, 0)

        core = lax.axis_index("box") % cores
        owner = read_table // boxes
        target = (owner % cores != core) * half + owner // cores * boxes + read_table % boxes

        steps = wedges // GROUP
        per = steps // wedge_groups
        sel, pick, tcat = pl.pallas_call(
            selector_kernel,
            grid=(steps,),
            in_specs=[
                pl.BlockSpec((1, boxes, GROUP * length), lambda i: (i // per, 0, i % per)),
                pl.BlockSpec((1, slots), lambda i: (0, 0)),
                pl.BlockSpec((length, c, c), lambda i: (0, 0, 0)),
            ],
            out_specs=[
                pl.BlockSpec((GROUP, length // 2 * boxes, 2 * slots), lambda i: (i, 0, 0)),
                pl.BlockSpec((slots, 2 * half), lambda i: (0, 0)),
                pl.BlockSpec((length * c, c), lambda i: (0, 0)),
            ],
            out_shape=[
                jax.ShapeDtypeStruct((wedges, length // 2 * boxes, 2 * slots), BF),
                jax.ShapeDtypeStruct((slots, 2 * half), BF),
                jax.ShapeDtypeStruct((length * c, c), BF),
            ],
            compiler_params=pltpu.CompilerParams(vmem_limit_bytes=16 << 20),
            name="selectors",
        )(spread, target, trans_ops)

        far = lax.ppermute(near, "box", swap)

        out = pl.pallas_call(
            main_kernel,
            grid=(steps,),
            in_specs=[
                pl.BlockSpec((half, p), lambda i: (0, 0)),
                pl.BlockSpec((half, p), lambda i: (0, 0)),
                pl.BlockSpec((slots, 2 * half), lambda i: (0, 0)),
                pl.BlockSpec((GROUP, length // 2 * boxes, 2 * slots), lambda i: (i, 0, 0)),
                pl.BlockSpec((GROUP, c, p), lambda i: (i, 0, 0)),
                pl.BlockSpec((length * c, c), lambda i: (0, 0)),
                pl.BlockSpec((GROUP, p, c), lambda i: (i, 0, 0)),
            ],
            out_specs=pl.BlockSpec((boxes, p), lambda i: (0, 0)),
            out_shape=jax.ShapeDtypeStruct((boxes, p), BF),
            scratch_shapes=[
                pltpu.VMEM((slots, p), BF),
                pltpu.VMEM((GROUP, 2 * slots, 2 * c), BF),
                pltpu.VMEM((GROUP * boxes, length * c), BF),
                pltpu.VMEM((boxes, p), F32),
            ],
            compiler_params=pltpu.CompilerParams(vmem_limit_bytes=24 << 20),
            name="main",
        )(near, far, pick, sel, up_ops, tcat, down_ops)
        return out.reshape(boxes, 1, p)

    in_specs = (P("box", "wedge", None), P(), P(), P(), P("box", None), P("box", "wedge", None))
    out_specs = P("box", "wedge", None)
    return jax.shard_map(body, mesh=mesh, in_specs=in_specs, out_specs=out_specs, check_vma=False)
```

time: 201 us -> 70.1 us (0.35)
  waiting for transfers between devices: 89.2 us -> 3.98 us
  local copies, waits for them, and re-layouts: 43.9 us -> 6.93 us
  Pallas kernels: 0 us -> 28.8 us
  matrix products: 26 us -> 0 us
  starting transfers between devices: 23.9 us -> 7.9 us
  blocking collectives: 14.9 us -> 21.3 us
    all_to_all x3 -> x1, waiting for transfers between devices: 89.2 us -> 3.98 us  [body(): spread = lax.all_to_all(spread, 'wedge', 0, 0)]
    pallas_call x0 -> x3, Pallas kernels: none -> 28.8 us  [the longest x1 17 us: body(): pl.pallas_call(main_kernel, grid=(steps,), in_specs=[pl.BlockSpec((half,...]
    dot_general x4 -> x0, matrix products: 26 us -> none  [the longest x1 13.2 us: body(): jnp.einsum('wbkfc,kdc->wbfd', sources, trans_ops, preferred_element_type=...]
    all_to_all x3 -> x1, starting transfers between devices: 23.9 us -> 4.18 us  [body(): spread = lax.all_to_all(spread, 'wedge', 0, 0)]
    reshape x1 -> x0, local copies, waits for them, and re-layouts: 18.2 us -> none  [body(): sources = sources.reshape(wedge_here, boxes_here, list_len, fields, coeffs)]
    gather x2 -> x0, local copies, waits for them, and re-layouts: 8.94 us -> none  [body(): picked = equivalents[local_ids]]
    all_to_all x4 -> x0, local copies, waits for them, and re-layouts: 8.33 us -> none  [the longest x1 5.19 us: body(): lax.all_to_all(picked, 'box', split_axis=0, concat_axis=0, tiled=True)]
    all_to_all x1, blocking collectives: 14.9 us -> 21.3 us  [body(): lax.all_to_all(copies, 'box', 0, 0, axis_index_groups=groups)]
  transfers between devices with their start and end apart: 3 -> 2, of which waited for: 3 -> 1; matrix products, arithmetic and copies ran while one was open for 3% -> 3% of each run, Pallas kernels for 0% -> 17%
where the time goes in v1:
time: 70.1 us; the launch traced here: 69.7 us
  Pallas kernels  28.8 us (41%)
  blocking collectives  21.3 us (30%)
  starting transfers between devices  7.9 us (11%)
  local copies, waits for them, and re-layouts  6.93 us (10%)
  waiting for transfers between devices  3.98 us (6%)
    all_to_all x1, blocking collectives, body(): lax.all_to_all(copies, 'box', 0, 0, axis_index_groups=groups)  21.3 us
    pallas_call x1, Pallas kernels, body(): pl.pallas_call(main_kernel, grid=(steps,), in_specs=[pl.BlockSpec((half,...  17 us
    pallas_call x1, Pallas kernels, body(): pl.pallas_call(selector_kernel, grid=(steps,), in_specs=[pl.BlockSpec((1,...  10.2 us
    unnamed x6, local copies, waits for them, and re-layouts  4.82 us
    all_to_all x1, starting transfers between devices, body(): spread = lax.all_to_all(spread, 'wedge', 0, 0)  4.18 us
    all_to_all x1, waiting for transfers between devices, body(): spread = lax.all_to_all(spread, 'wedge', 0, 0)  3.98 us
    ppermute x1, starting transfers between devices, body(): far = lax.ppermute(near, 'box', swap)  3.72 us
    pallas_call x1, Pallas kernels, body(): pl.pallas_call(columns_kernel, out_shape=jax.ShapeDtypeStruct((boxes, wed...  1.6 us
  transfers between devices with their start and end apart: 2, of which 1 were waited for; matrix products, arithmetic and copies ran while one was open for 3% of the time, Pallas kernels for 17%

profile of v1, /device:TPU:1, one launch (start us, length us, event | category | flops | bytes accessed | tf_op | source)
XLA Modules:
  0.0 69.7 jit_solution(1399024302751764820)
XLA Ops:
  0.0 0.7 %broadcast_in_dim.14 = bf16[32,32,128]{2,1,0:T(8,128)(2,1)S(1)} broadcast(bf16[32,128]{1,0:T(8,128)(2,1)} %bitcast.7), dimensions={1,2} | broadcast | bytes 270336 | tf_op jit(solution)/shard_map/broadcast_in_dim | solution.py:103
  0.7 21.3 %all_to_all.10 = bf16[32,32,128]{2,1,0:T(8,128)(2,1)S(1)} all-to-all(bf16[32,32,128]{2,1,0:T(8,128)(2,1)S(1)} %broadcast_in_dim.14), channel_id=1, replica_groups={{0,2,4,6,8,10,12,14,16,18,20,22,24,26,28,30,32,34,36,38,40,42,44,46,48,..., dimensions={0} | all-to-all | bytes 524288 | tf_op jit(solution)/shard_map/all_to_all | solution.py:104
  22.1 3.7 %collective-permute-start = (bf16[1024,128]{1,0:T(8,128)(2,1)S(1)}, bf16[1024,128]{1,0:T(8,128)(2,1)S(1)}, u32[]{:S(2)}, u32[]{:S(2)}) collective-permute-start(bf16[1024,128]{1,0:T(8,128)(2,1)S(1)} %bitcast.4), channel_id=1, source_target_pairs={{0,1},{1,0},{2,3},{3,2},{4,5},{5,4},{6,7},{7,6},{8,9},{9,8},{10,11... | collective-permute-start | bytes 786440 | tf_op jit(solution)/shard_map/ppermute | solution.py:143
  25.8 1.6 %columns.1 = bf16[32,384]{1,0:T(8,128)(2,1)} custom-call(s32[24,16,32]{2,1,0:T(8,128)} %bitcast.6), custom_call_target="tpu_custom_call" | custom-call | tf_op jit(solution)/shard_map/columns/pallas_call | solution.py:107
  27.4 1.4 %broadcast_in_dim.15 = bf16[4,32,384]{2,1,0:T(8,128)(2,1)} broadcast(bf16[32,384]{1,0:T(8,128)(2,1)} %columns.1), dimensions={1,2} | broadcast | bytes 122880 | tf_op jit(solution)/shard_map/broadcast_in_dim | solution.py:112
  28.8 4.2 %all-to-all-start.1 = ((bf16[4,32,384]{2,1,0:T(8,128)(2,1)}), bf16[4,32,384]{2,1,0:T(8,128)(2,1)S(1)}, u32[]{:S(2)}, u32[]{:S(2)}) async-start(bf16[4,32,384]{2,1,0:T(8,128)(2,1)} %broadcast_in_dim.15), calls=%async_computation.1 | async-start | bytes 196608 | tf_op jit(solution)/shard_map/all_to_all | solution.py:113
  33.0 0.7 fusion.target_ref
  33.6 4.0 %all-to-all-done.1.columns_ref = bf16[4,32,384]{2,1,0:T(8,128)(2,1)S(1)} async-done(((bf16[4,32,384]{2,1,0:T(8,128)(2,1)}), bf16[4,32,384]{2,1,0:T(8,128)(2,1)S(1)}, u32[]{:S(2)}, u32[]{:S(2)}) %all-to-all-start.1) | async-done | bytes 98336 | tf_op jit(solution)/shard_map/all_to_all | solution.py:113
  37.6 0.0 copy-start.2
  37.6 1.0 %copy-done.2 = bf16[16,128,128]{2,1,0:T(8,128)(2,1)S(1)} copy-done((bf16[16,128,128]{2,1,0:T(8,128)(2,1)S(1)}, bf16[16,128,128]{2,1,0:T(8,128)(2,1)}, u32[]{:S(2)}) %copy-start.2) | copy-done | bytes 524312
  38.7 10.2 %selectors.1 = (bf16[96,256,256]{2,1,0:T(8,128)(2,1)S(1)}, bf16[128,2048]{1,0:T(8,128)(2,1)S(1)}, bf16[2048,128]{1,0:T(8,128)(2,1)S(1)}) custom-call(bf16[4,32,384]{2,1,0:T(8,128)(2,1)S(1)} %all-to-all-done.1.columns_ref, s32[1,128]{1,0:T(1,128)S(1)} %fusion.target_ref, bf16[16,128,128]{2,1,0:T(8,128)(2,1)S(1)} %copy-done.2), custom_call_target="tpu_custom_call" | custom-call | tf_op jit(solution)/shard_map/selectors/pallas_call | solution.py:121
  48.9 0.0 collective-permute-done.far_ref
  48.9 0.0 copy-start
  48.9 1.9 %copy-done = bf16[96,128,128]{2,1,0:T(8,128)(2,1)S(1)} copy-done((bf16[96,128,128]{2,1,0:T(8,128)(2,1)S(1)}, bf16[96,128,128]{2,1,0:T(8,128)(2,1)}, u32[]{:S(2)}) %copy-start) | copy-done | bytes 3145752
  50.8 0.0 copy-start.1
  50.8 1.9 %copy-done.1 = bf16[96,128,128]{2,1,0:T(8,128)(2,1)S(1)} copy-done((bf16[96,128,128]{2,1,0:T(8,128)(2,1)S(1)}, bf16[96,128,128]{2,1,0:T(8,128)(2,1)}, u32[]{:S(2)}) %copy-start.1) | copy-done | bytes 3145752
  52.7 17.0 %main.1 = bf16[32,128]{1,0:T(8,128)(2,1)} custom-call(bf16[1024,128]{1,0:T(8,128)(2,1)S(1)} %bitcast.5, bf16[1024,128]{1,0:T(8,128)(2,1)S(1)} %collective-permute-done.far_ref, bf16[128,2048]{1,0:T(8,128)(2,1)S(1)} %get-tuple-element.8.pick_ref, bf16[96,256,256]{2,1,0:T(8,128)(2,1)S(1)} %get-tuple-element.9.sel_ref, bf16[96,128,128]{2,1,0:T(8,128)(2,1)S(1)} %copy-done, ...), custom_call_target="tpu_custom_call" | custom-call | tf_op jit(solution)/shard_map/main/pallas_call | solution.py:145
Async XLA Ops:
  22.1 26.8 %collective-permute-start = (bf16[1024,128]{1,0:T(8,128)(2,1)S(1)}, bf16[1024,128]{1,0:T(8,128)(2,1)S(1)}, u32[]{:S(2)}, u32[]{:S(2)}) collective-permute-start(bf16[1024,128]{1,0:T(8,128)(2,1)S(1)} %bitcast.4), channel_id=1, source_target_pairs={{0,1},{1,0},{2,3},{3,2},{4,5},{5,4},{6,7},{7,6},{8,9},{9,8},{10,11... | collective-permute-start | bytes 786440 | tf_op jit(solution)/shard_map/ppermute | solution.py:143
  28.8 8.8 %all-to-all-start.1 = ((bf16[4,32,384]{2,1,0:T(8,128)(2,1)}), bf16[4,32,384]{2,1,0:T(8,128)(2,1)S(1)}, u32[]{:S(2)}, u32[]{:S(2)}) async-start(bf16[4,32,384]{2,1,0:T(8,128)(2,1)} %broadcast_in_dim.15), calls=%async_computation.1 | async-start | bytes 196608 | tf_op jit(solution)/shard_map/all_to_all | solution.py:113
  37.6 1.0 %copy-start.2 = (bf16[16,128,128]{2,1,0:T(8,128)(2,1)S(1)}, bf16[16,128,128]{2,1,0:T(8,128)(2,1)}, u32[]{:S(2)}) copy-start(bf16[16,128,128]{2,1,0:T(8,128)(2,1)} %trans_ref.1) | copy-start | bytes 1572868
  48.9 1.9 %copy-start = (bf16[96,128,128]{2,1,0:T(8,128)(2,1)S(1)}, bf16[96,128,128]{2,1,0:T(8,128)(2,1)}, u32[]{:S(2)}) copy-start(bf16[96,128,128]{2,1,0:T(8,128)(2,1)} %up_ref.1) | copy-start | bytes 9437188
  50.8 1.9 %copy-start.1 = (bf16[96,128,128]{2,1,0:T(8,128)(2,1)S(1)}, bf16[96,128,128]{2,1,0:T(8,128)(2,1)}, u32[]{:S(2)}) copy-start(bf16[96,128,128]{2,1,0:T(8,128)(2,1)} %down_ref.1) | copy-start | bytes 9437188

commit v2 on v0

v2 whole, which is shorter than its diff:
```python
import functools

import jax
import jax.numpy as jnp
from jax import lax
from jax.experimental import pallas as pl
from jax.experimental.pallas import tpu as pltpu
from jax.sharding import PartitionSpec as P


BF = jnp.bfloat16
F32 = jnp.float32
NT = (((1,), (1,)), ((), ()))
GROUP = 8
VMEM = pl.BlockSpec(memory_space=pltpu.VMEM)
SMEM = pl.BlockSpec(memory_space=pltpu.SMEM)
HBM = pl.BlockSpec(memory_space=pltpu.HBM)


def pack_kernel(list_ref, out_ref):
    length, boxes = list_ref.shape[1:]
    for k in range(length):
        out_ref[:, k * boxes : (k + 1) * boxes] = list_ref[:, k, :].astype(F32).astype(BF)


def table_kernel(place_ref, table_ref, trans_ref, *refs):
    list_refs, (pick_ref, tcat_ref, lists_ref) = refs[:-3], refs[-3:]
    here = list_refs[0].shape[0]
    for n, ref in enumerate(list_refs):
        lists_ref[n * here : (n + 1) * here, :] = ref[...].astype(F32)
    slots = table_ref.shape[1]
    length, c, _ = trans_ref.shape
    half = pick_ref.shape[1] // 2
    table = table_ref[...]
    owner = table >> 5
    other = (owner & 1) != place_ref[0]
    target = jnp.where(other, half, 0) + ((owner >> 1) << 5) + (table & 31)
    spread = jnp.broadcast_to(target.astype(F32), (slots, slots)).T
    number = lax.broadcasted_iota(jnp.int32, (slots, slots), 1).astype(F32)
    for j in range(2 * half // slots):
        pick_ref[:, j * slots : (j + 1) * slots] = jnp.where(spread == number + float(j * slots), 1.0, 0.0).astype(BF)
    for k in range(length):
        at = (k % (length // 2)) * 2 * c + k // (length // 2) * c
        tcat_ref[at : at + c, :] = trans_ref[k].T


def main_kernel(
    pieces, place_ref, near_ref, far_ref, pick_ref, tcat_ref, lists, up_hbm, down_hbm, out_ref,
    dens, blocks, sel, wide, up, down, sems,
):
    wedges, c, p = up.shape
    half = near_ref.shape[0]
    slots = pick_ref.shape[0]
    boxes = out_ref.shape[0]
    pairs = sel.shape[2] // boxes
    here = wedges // pieces
    steps = wedges // GROUP
    per = here // GROUP

    def fetch(hbm, held, kind, i):
        group = lax.rem(place_ref[1] + pieces - i // per, pieces)
        source = pl.ds(pl.multiple_of(group * here + i % per * GROUP, GROUP), GROUP)
        return pltpu.make_async_copy(hbm.at[source], held.at[pl.ds(i * GROUP, GROUP)], sems.at[kind, i])

    def fetch_up(i):
        return fetch(up_hbm, up, 0, i)

    def fetch_down(i):
        return fetch(down_hbm, down, 1, i)

    for i in range(steps):
        fetch_up(i).start()
        fetch_down(i).start()

    blocks[...] = jnp.zeros_like(blocks)
    number = lax.broadcasted_iota(jnp.int32, (slots, slots), 0).astype(F32)
    chunks = lists.shape[1] // slots

    def rows_of(i):
        return lists[pl.ds(pl.multiple_of(i * GROUP, GROUP), GROUP), :]

    def select(rows, slot, w):
        for j in range(chunks):
            row = jnp.broadcast_to(rows[w : w + 1, j * slots : (j + 1) * slots], (slots, slots))
            hit = jnp.where(row == number, 1.0, 0.0).astype(BF)
            top, left = j % (chunks // 2) * slots, j // (chunks // 2) * slots
            sel[slot, w, top : top + slots, left : left + slots] = hit.T

    def equivalents(i, slot):
        maps = up[pl.ds(pl.multiple_of(i * GROUP, GROUP), GROUP)].reshape(GROUP * c, p)
        value = lax.dot_general(dens[...], maps, NT, preferred_element_type=F32).astype(BF)
        for w in range(GROUP):
            one = value[:, w * c : (w + 1) * c]
            blocks[slot, w, :slots, :c] = one
            blocks[slot, w, slots:, c:] = one

    rows = rows_of(0)
    for w in range(GROUP):
        select(rows, 0, w)
    picked = jnp.dot(pick_ref[:, :half], near_ref[...], preferred_element_type=F32)
    picked += jnp.dot(pick_ref[:, half:], far_ref[...], preferred_element_type=F32)
    dens[...] = picked.astype(BF)
    fetch_up(0).wait()
    equivalents(0, 0)

    def step(b, total):
        first = b * 2
        fetch_up(first + 1).wait()
        fetch_down(first).wait()
        fetch_down(first + 1).wait()

        @pl.when(b < steps // 2 - 1)
        def _():
            fetch_up(first + 2).wait()

        for h in (0, 1):
            now = first + h
            later = lax.rem(now + 1, steps)
            rows = rows_of(later)
            for w in range(GROUP):
                sources = jnp.dot(sel[h, w], blocks[h, w], preferred_element_type=F32).astype(BF)
                for j in range(pairs):
                    wide[h, w * boxes : (w + 1) * boxes, j * 2 * c : (j + 1) * 2 * c] = (
                        sources[j * boxes : (j + 1) * boxes]
                    )
                select(rows, 1 - h, w)
            equivalents(later, 1 - h)
            local = jnp.dot(wide[h], tcat_ref[...], preferred_element_type=F32).astype(BF)
            flat = jnp.concatenate([local[w * boxes : (w + 1) * boxes] for w in range(GROUP)], 1)
            maps = jnp.concatenate([down[now * GROUP + w] for w in range(GROUP)], 1)
            total = total + lax.dot_general(flat, maps, NT, preferred_element_type=F32)
        return total

    total = lax.fori_loop(0, steps // 2, step, jnp.zeros((boxes, p), F32))
    out_ref[...] = total.astype(BF)


def solution(mesh):
    x_chips, z_chips, cores = 4, 8, 2
    groups = [[(x * z_chips + z) * cores + c for x in range(x_chips) for z in range(z_chips)] for c in range(cores)]
    swap = [(i, i ^ 1) for i in range(x_chips * z_chips * cores)]

    def parts(densities, up_ops, trans_ops, down_ops, read_table, interaction):
        boxes, _, p = densities.shape
        wedges, c, _ = up_ops.shape
        wedge_here, length = interaction.shape[1:]
        wedge_groups = wedges // wedge_here
        slots = read_table.shape[1]
        chips = len(groups[0])
        half = chips * boxes
        width = length * boxes

        copies = jnp.broadcast_to(densities.reshape(1, boxes, p), (chips, boxes, p))
        near = lax.all_to_all(copies, "box", 0, 0, axis_index_groups=groups)
        near = near.reshape(half, p)

        lists = pl.pallas_call(
            pack_kernel,
            in_specs=[VMEM],
            out_specs=VMEM,
            out_shape=jax.ShapeDtypeStruct((wedge_here, width), BF),
            compiler_params=pltpu.CompilerParams(vmem_limit_bytes=4 << 20),
            name="pack",
        )(interaction.transpose(1, 2, 0))
        spread = [lists]
        for j in range(1, wedge_groups):
            spread.append(lax.ppermute(lists, "wedge", [(i, (i + j) % wedge_groups) for i in range(wedge_groups)]))
        place = jnp.stack([lax.axis_index("box") % cores, lax.axis_index("wedge")])

        pick, tcat, lists = pl.pallas_call(
            table_kernel,
            in_specs=[SMEM] + [VMEM] * (2 + wedge_groups),
            out_specs=[VMEM] * 3,
            out_shape=[
                jax.ShapeDtypeStruct((slots, 2 * half), BF),
                jax.ShapeDtypeStruct((length * c, c), BF),
                jax.ShapeDtypeStruct((wedges, width), F32),
            ],
            compiler_params=pltpu.CompilerParams(vmem_limit_bytes=4 << 20),
            name="tables",
        )(place, read_table, trans_ops, *spread)

        far = lax.ppermute(near, "box", swap)

        out = pl.pallas_call(
            functools.partial(main_kernel, wedge_groups),
            in_specs=[SMEM] + [VMEM] * 5 + [HBM, HBM],
            out_specs=VMEM,
            out_shape=jax.ShapeDtypeStruct((boxes, p), BF),
            scratch_shapes=[
                pltpu.VMEM((slots, p), BF),
                pltpu.VMEM((2, GROUP, 2 * slots, 2 * c), BF),
                pltpu.VMEM((2, GROUP, length // 2 * boxes, 2 * slots), BF),
                pltpu.VMEM((2, GROUP * boxes, length * c), BF),
                pltpu.VMEM((wedges, c, p), BF),
                pltpu.VMEM((wedges, p, c), BF),
                pltpu.SemaphoreType.DMA((2, wedges // GROUP)),
            ],
            compiler_params=pltpu.CompilerParams(vmem_limit_bytes=40 << 20),
            name="main",
        )(place, near, far, pick, tcat, lists, pltpu.with_memory_space_constraint(up_ops, pltpu.HBM), pltpu.with_memory_space_constraint(down_ops, pltpu.HBM))
        return out.reshape(boxes, 1, p)

    in_specs = (P("box", "wedge", None), P(), P(), P(), P("box", None), P("box", "wedge", None))
    out_specs = P("box", "wedge", None)
    return jax.shard_map(parts, mesh=mesh, in_specs=in_specs, out_specs=out_specs, check_vma=False)
```

time: 201 us -> 50.1 us (0.25)
  waiting for transfers between devices: 89.2 us -> 1.53 us
  local copies, waits for them, and re-layouts: 43.9 us -> 3.35 us
  matrix products: 26 us -> 0 us
  starting transfers between devices: 23.9 us -> 8.78 us
  Pallas kernels: 0 us -> 14.8 us
  blocking collectives: 14.9 us -> 21.3 us
    all_to_all x3 -> x0, waiting for transfers between devices: 89.2 us -> none  [the longest x1 71.5 us: body(): lax.all_to_all(picked, 'box', split_axis=0, concat_axis=0, tiled=True)]
    dot_general x4 -> x0, matrix products: 26 us -> none  [the longest x1 13.2 us: body(): jnp.einsum('wbkfc,kdc->wbfd', sources, trans_ops, preferred_element_type=...]
    all_to_all x3 -> x0, starting transfers between devices: 23.9 us -> none  [the longest x1 13 us: body(): lax.all_to_all(read_table.reshape(box_groups, per_owner), 'box', split_ax...]
    reshape x1 -> x0, local copies, waits for them, and re-layouts: 18.2 us -> none  [body(): sources = sources.reshape(wedge_here, boxes_here, list_len, fields, coeffs)]
    pallas_call x0 -> x3, Pallas kernels: none -> 14.8 us  [the longest x1 13.7 us: parts(): pl.pallas_call(functools.partial(main_kernel, wedge_groups), in_specs=[SM...]
    gather x2 -> x0, local copies, waits for them, and re-layouts: 8.94 us -> none  [body(): picked = equivalents[local_ids]]
    ppermute x0 -> x4, starting transfers between devices: none -> 8.78 us  [the longest x3 5.06 us: parts(): lax.ppermute(lists, 'wedge', [(i, (i + j) % wedge_groups) for i in range(...]
    all_to_all x4 -> x0, local copies, waits for them, and re-layouts: 8.33 us -> none  [the longest x1 5.19 us: body(): lax.all_to_all(picked, 'box', split_axis=0, concat_axis=0, tiled=True)]
  transfers between devices with their start and end apart: 3 -> 4, of which waited for: 3 -> 2; matrix products, arithmetic and copies ran while one was open for 3% -> 0% of each run, Pallas kernels for 0% -> 2%
where the time goes in v2:
time: 50.1 us; the launch traced here: 49.9 us
  blocking collectives  21.3 us (43%)
  Pallas kernels  14.8 us (30%)
  starting transfers between devices  8.78 us (18%)
  local copies, waits for them, and re-layouts  3.35 us (7%)
  waiting for transfers between devices  1.53 us (3%)
    all_to_all x1, blocking collectives, parts(): near = lax.all_to_all(copies, 'box', 0, 0, axis_index_groups=groups)  21.3 us
    pallas_call x1, Pallas kernels, parts(): pl.pallas_call(functools.partial(main_kernel, wedge_groups), in_specs=[SM...  13.7 us
    ppermute x3, starting transfers between devices, parts(): lax.ppermute(lists, 'wedge', [(i, (i + j) % wedge_groups) for i in range(...  5.06 us
    ppermute x1, starting transfers between devices, parts(): far = lax.ppermute(near, 'box', swap)  3.72 us
    unnamed x6, local copies, waits for them, and re-layouts  2.62 us
    ppermute x3, waiting for transfers between devices, parts(): lax.ppermute(lists, 'wedge', [(i, (i + j) % wedge_groups) for i in range(...  1.53 us
  transfers between devices with their start and end apart: 4, of which 2 were waited for; matrix products, arithmetic and copies ran while one was open for 0% of the time, Pallas kernels for 2%

profile of v2, /device:TPU:1, one launch (start us, length us, event | category | flops | bytes accessed | tf_op | source)
XLA Modules:
  0.0 49.9 jit_solution(12554051028643925457)
XLA Ops:
  0.0 0.7 %broadcast_in_dim.8 = bf16[32,32,128]{2,1,0:T(8,128)(2,1)S(1)} broadcast(bf16[32,128]{1,0:T(8,128)(2,1)} %bitcast.9), dimensions={1,2} | broadcast | bytes 270336 | tf_op jit(solution)/shard_map/broadcast_in_dim | solution.py:153
  0.7 21.3 %all_to_all.5 = bf16[32,32,128]{2,1,0:T(8,128)(2,1)S(1)} all-to-all(bf16[32,32,128]{2,1,0:T(8,128)(2,1)S(1)} %broadcast_in_dim.8), channel_id=1, replica_groups={{0,2,4,6,8,10,12,14,16,18,20,22,24,26,28,30,32,34,36,38,40,42,44,46,48,..., dimensions={0} | all-to-all | bytes 524288 | tf_op jit(solution)/shard_map/all_to_all | solution.py:154
  22.1 3.7 %collective-permute-start = (bf16[1024,128]{1,0:T(8,128)(2,1)S(1)}, bf16[1024,128]{1,0:T(8,128)(2,1)S(1)}, u32[]{:S(2)}, u32[]{:S(2)}) collective-permute-start(bf16[1024,128]{1,0:T(8,128)(2,1)S(1)} %bitcast.6), channel_id=1, source_target_pairs={{0,1},{1,0},{2,3},{3,2},{4,5},{5,4},{6,7},{7,6},{8,9},{9,8},{10,11... | collective-permute-start | bytes 786440 | tf_op jit(solution)/shard_map/ppermute | solution.py:183
  25.8 0.0 copy-start.1
  25.8 0.9 %copy-done.1 = s32[32,24,16]{0,2,1:T(8,128)S(1)} copy-done((s32[32,24,16]{0,2,1:T(8,128)S(1)}, s32[32,24,16]{0,2,1:T(8,128)}, u32[]{:S(2)}) %copy-start.1) | copy-done | bytes 49176
  26.7 0.3 pack.1.refs_0_
  27.0 1.4 %collective-permute-start.1 = (bf16[24,512]{1,0:T(8,128)(2,1)S(1)}, bf16[24,512]{1,0:T(8,128)(2,1)S(1)}, u32[]{:S(2)}, u32[]{:S(2)}) collective-permute-start(bf16[24,512]{1,0:T(8,128)(2,1)S(1)} %pack.1.refs_0_), channel_id=1, source_target_pairs={{0,64},{64,128},{128,192},{192,0},{1,65},{65,129},{129,193},{193,1... | collective-permute-start | bytes 73736 | tf_op jit(solution)/shard_map/ppermute | solution.py:167
  28.3 2.6 %collective-permute-start.2 = (bf16[24,512]{1,0:T(8,128)(2,1)S(1)}, bf16[24,512]{1,0:T(8,128)(2,1)S(1)}, u32[]{:S(2)}, u32[]{:S(2)}) collective-permute-start(bf16[24,512]{1,0:T(8,128)(2,1)S(1)} %pack.1.refs_0_), channel_id=1, source_target_pairs={{0,128},{64,192},{128,0},{192,64},{1,129},{65,193},{129,1},{193,65... | collective-permute-start | bytes 73736 | tf_op jit(solution)/shard_map/ppermute | solution.py:167
  31.0 1.1 %collective-permute-start.3 = (bf16[24,512]{1,0:T(8,128)(2,1)S(1)}, bf16[24,512]{1,0:T(8,128)(2,1)S(1)}, u32[]{:S(2)}, u32[]{:S(2)}) collective-permute-start(bf16[24,512]{1,0:T(8,128)(2,1)S(1)} %pack.1.refs_0_), channel_id=1, source_target_pairs={{0,192},{64,0},{128,64},{192,128},{1,193},{65,1},{129,65},{193,129... | collective-permute-start | bytes 73736 | tf_op jit(solution)/shard_map/ppermute | solution.py:167
  32.0 0.1 pad_add_fusion.place_ref
  32.1 0.0 collective-permute-done.1.refs_1_
  32.1 0.6 %collective-permute-done.2.refs_2_ = bf16[24,512]{1,0:T(8,128)(2,1)S(1)} collective-permute-done((bf16[24,512]{1,0:T(8,128)(2,1)S(1)}, bf16[24,512]{1,0:T(8,128)(2,1)S(1)}, u32[]{:S(2)}, u32[]{:S(2)}) %collective-permute-start.2) | collective-permute-done | bytes 24608 | tf_op jit(solution)/shard_map/ppermute | solution.py:167
  32.7 1.0 %collective-permute-done.3.refs_3_ = bf16[24,512]{1,0:T(8,128)(2,1)S(1)} collective-permute-done((bf16[24,512]{1,0:T(8,128)(2,1)S(1)}, bf16[24,512]{1,0:T(8,128)(2,1)S(1)}, u32[]{:S(2)}, u32[]{:S(2)}) %collective-permute-start.3) | collective-permute-done | bytes 24608 | tf_op jit(solution)/shard_map/ppermute | solution.py:167
  33.6 0.0 copy-start
  33.7 1.0 %copy-done = bf16[16,128,128]{2,1,0:T(8,128)(2,1)S(1)} copy-done((bf16[16,128,128]{2,1,0:T(8,128)(2,1)S(1)}, bf16[16,128,128]{2,1,0:T(8,128)(2,1)}, u32[]{:S(2)}) %copy-start) | copy-done | bytes 524312
  34.7 0.0 copy-start.2
  34.7 0.7 %copy-done.2 = s32[1,128]{1,0:T(1,128)S(1)} copy-done((s32[1,128]{1,0:T(1,128)S(1)}, s32[1,128]{1,0:T(1,128)}, u32[]{:S(2)}) %copy-start.2) | copy-done | bytes 536
  35.3 0.8 %tables.1 = (bf16[128,2048]{1,0:T(8,128)(2,1)S(1)}, bf16[2048,128]{1,0:T(8,128)(2,1)S(1)}, f32[96,512]{1,0:T(8,128)S(1)}) custom-call(s32[2]{0:T(128)S(1)} %pad_add_fusion.place_ref, s32[1,128]{1,0:T(1,128)S(1)} %copy-done.2, bf16[16,128,128]{2,1,0:T(8,128)(2,1)S(1)} %copy-done, bf16[24,512]{1,0:T(8,128)(2,1)S(1)} %pack.1.refs_0_, ...), custom_call_target="tpu_custom_call" | custom-call | tf_op jit(solution)/shard_map/tables/pallas_call | solution.py:170
  36.2 0.0 collective-permute-done.far_ref
  36.2 13.7 %main.1 = bf16[32,128]{1,0:T(8,128)(2,1)} custom-call(s32[2]{0:T(128)S(1)} %pad_add_fusion.place_ref, bf16[1024,128]{1,0:T(8,128)(2,1)S(1)} %bitcast.7, bf16[1024,128]{1,0:T(8,128)(2,1)S(1)} %collective-permute-done.far_ref, bf16[128,2048]{1,0:T(8,128)(2,1)S(1)} %get-tuple-element.8.pick_ref, bf16[2048,128]{1,0:T(8,128)(2,1)S(1)} %get-tuple-element.9.tcat_ref, ...), custom_call_target="tpu_custom_call" | custom-call | tf_op jit(solution)/shard_map/main/pallas_call | solution.py:185
Async XLA Ops:
  22.1 14.1 %collective-permute-start = (bf16[1024,128]{1,0:T(8,128)(2,1)S(1)}, bf16[1024,128]{1,0:T(8,128)(2,1)S(1)}, u32[]{:S(2)}, u32[]{:S(2)}) collective-permute-start(bf16[1024,128]{1,0:T(8,128)(2,1)S(1)} %bitcast.6), channel_id=1, source_target_pairs={{0,1},{1,0},{2,3},{3,2},{4,5},{5,4},{6,7},{7,6},{8,9},{9,8},{10,11... | collective-permute-start | bytes 786440 | tf_op jit(solution)/shard_map/ppermute | solution.py:183
  25.8 0.9 %copy-start.1 = (s32[32,24,16]{0,2,1:T(8,128)S(1)}, s32[32,24,16]{0,2,1:T(8,128)}, u32[]{:S(2)}) copy-start(s32[32,24,16]{0,2,1:T(8,128)} %param.11) | copy-start | bytes 147460
  27.0 5.1 %collective-permute-start.1 = (bf16[24,512]{1,0:T(8,128)(2,1)S(1)}, bf16[24,512]{1,0:T(8,128)(2,1)S(1)}, u32[]{:S(2)}, u32[]{:S(2)}) collective-permute-start(bf16[24,512]{1,0:T(8,128)(2,1)S(1)} %pack.1.refs_0_), channel_id=1, source_target_pairs={{0,64},{64,128},{128,192},{192,0},{1,65},{65,129},{129,193},{193,1... | collective-permute-start | bytes 73736 | tf_op jit(solution)/shard_map/ppermute | solution.py:167
  28.3 4.3 %collective-permute-start.2 = (bf16[24,512]{1,0:T(8,128)(2,1)S(1)}, bf16[24,512]{1,0:T(8,128)(2,1)S(1)}, u32[]{:S(2)}, u32[]{:S(2)}) collective-permute-start(bf16[24,512]{1,0:T(8,128)(2,1)S(1)} %pack.1.refs_0_), channel_id=1, source_target_pairs={{0,128},{64,192},{128,0},{192,64},{1,129},{65,193},{129,1},{193,65... | collective-permute-start | bytes 73736 | tf_op jit(solution)/shard_map/ppermute | solution.py:167
  31.0 2.7 %collective-permute-start.3 = (bf16[24,512]{1,0:T(8,128)(2,1)S(1)}, bf16[24,512]{1,0:T(8,128)(2,1)S(1)}, u32[]{:S(2)}, u32[]{:S(2)}) collective-permute-start(bf16[24,512]{1,0:T(8,128)(2,1)S(1)} %pack.1.refs_0_), channel_id=1, source_target_pairs={{0,192},{64,0},{128,64},{192,128},{1,193},{65,1},{129,65},{193,129... | collective-permute-start | bytes 73736 | tf_op jit(solution)/shard_map/ppermute | solution.py:167
  33.6 1.0 %copy-start = (bf16[16,128,128]{2,1,0:T(8,128)(2,1)S(1)}, bf16[16,128,128]{2,1,0:T(8,128)(2,1)}, u32[]{:S(2)}) copy-start(bf16[16,128,128]{2,1,0:T(8,128)(2,1)} %trans_ref.1) | copy-start | bytes 1572868
  34.7 0.7 %copy-start.2 = (s32[1,128]{1,0:T(1,128)S(1)}, s32[1,128]{1,0:T(1,128)}, u32[]{:S(2)}) copy-start(s32[1,128]{1,0:T(1,128)} %table_ref.1) | copy-start | bytes 1540

commit v3 on v2

v3 whole, which is shorter than its diff:
```python
import jax
import jax.numpy as jnp
from jax import lax
from jax.experimental import pallas as pl
from jax.experimental.pallas import tpu as pltpu
from jax.sharding import PartitionSpec as P


BF = jnp.bfloat16
F32 = jnp.float32
NT = (((1,), (1,)), ((), ()))
GROUP = 8
VMEM = pl.BlockSpec(memory_space=pltpu.VMEM)
SMEM = pl.BlockSpec(memory_space=pltpu.SMEM)
HBM = pl.BlockSpec(memory_space=pltpu.HBM)


def pack_kernel(list_ref, out_ref):
    length, boxes = list_ref.shape[1:]
    for k in range(length):
        out_ref[:, k * boxes : (k + 1) * boxes] = list_ref[:, k, :].astype(F32).astype(BF)


def table_kernel(place_ref, table_ref, trans_ref, pick_ref, tcat_ref):
    slots = table_ref.shape[1]
    length, c, _ = trans_ref.shape
    half = pick_ref.shape[1] // 2
    table = table_ref[...]
    owner = table >> 5
    other = (owner & 1) != place_ref[0]
    target = jnp.where(other, half, 0) + ((owner >> 1) << 5) + (table & 31)
    spread = jnp.broadcast_to(target.astype(F32), (slots, slots)).T
    number = lax.broadcasted_iota(jnp.int32, (slots, slots), 1).astype(F32)
    for j in range(2 * half // slots):
        pick_ref[:, j * slots : (j + 1) * slots] = jnp.where(spread == number + float(j * slots), 1.0, 0.0).astype(BF)
    for k in range(length):
        tcat_ref[k * c : (k + 1) * c, :] = trans_ref[k].T


def main_kernel(place_ref, near_ref, far_ref, pick_ref, tcat_ref, *refs):
    list_refs, (up_hbm, down_hbm, out_ref, lists, dens, blocks, sel, wide, held, up, down, sems) = refs[:-12], refs[-12:]
    wedges, c, p = up.shape
    half = near_ref.shape[0]
    slots = pick_ref.shape[0]
    boxes = out_ref.shape[0]
    length = tcat_ref.shape[0] // c
    pieces = len(list_refs)
    here = wedges // pieces
    steps = wedges // GROUP

    def fetch(hbm, ref, kind, piece, skip, count, at):
        group = lax.rem(place_ref[1] + pieces - piece, pieces)
        source = pl.ds(pl.multiple_of(group * here + skip, GROUP), count)
        return pltpu.make_async_copy(hbm.at[source], ref.at[pl.ds(piece * here + skip, count)], sems.at[kind, at])

    ups = [fetch(up_hbm, up, 0, 0, 0, GROUP, 0), fetch(up_hbm, up, 0, 0, GROUP, here - GROUP, 1)]
    ups += [fetch(up_hbm, up, 0, n, 0, here, n + 1) for n in range(1, pieces)]
    downs = [fetch(down_hbm, down, 1, n, 0, here, n) for n in range(pieces)]
    for copy in ups[:2] + downs[:1]:
        copy.start()
    for n in range(1, pieces):
        ups[n + 1].start()
        downs[n].start()

    for n, ref in enumerate(list_refs):
        lists[n * here : (n + 1) * here, :] = ref[...].astype(F32)
    blank = jnp.zeros((GROUP // 2, slots, c), BF)
    for slot in range(2):
        blocks[slot, :, :slots, c:] = blank
        blocks[slot, :, slots:, :c] = blank
    held[1] = jnp.zeros(held.shape[1:], BF)
    number = lax.broadcasted_iota(jnp.int32, (slots, slots), 0).astype(F32)
    chunks = lists.shape[1] // slots

    def rows_of(i):
        return lists[pl.ds(pl.multiple_of(i * GROUP, GROUP), GROUP), :]

    def select(rows, slot, w):
        for j in range(chunks):
            row = jnp.broadcast_to(rows[w : w + 1, j * slots : (j + 1) * slots], (slots, slots))
            hit = jnp.where(row == number, 1.0, 0.0).astype(BF)
            sel[slot, w // 2, j * slots : (j + 1) * slots, w % 2 * slots : (w % 2 + 1) * slots] = hit.T

    def equivalents(i, slot):
        maps = up[pl.ds(pl.multiple_of(i * GROUP, GROUP), GROUP)].reshape(GROUP * c, p)
        value = lax.dot_general(dens[...], maps, NT, preferred_element_type=F32).astype(BF)
        for w in range(GROUP):
            blocks[slot, w // 2, w % 2 * slots : (w % 2 + 1) * slots, w % 2 * c : (w % 2 + 1) * c] = (
                value[:, w * c : (w + 1) * c]
            )

    def gather(slot, pair):
        sources = jnp.dot(sel[slot, pair], blocks[slot, pair], preferred_element_type=F32).astype(BF)
        for k in range(length):
            for d in range(2):
                w = 2 * pair + d
                wide[slot, w * boxes : (w + 1) * boxes, k * c : (k + 1) * c] = (
                    sources[k * boxes : (k + 1) * boxes, d * c : (d + 1) * c]
                )

    def translate(slot):
        local = jnp.dot(wide[slot], tcat_ref[...], preferred_element_type=F32).astype(BF)
        for w in range(GROUP):
            held[slot, :, w * c : (w + 1) * c] = local[w * boxes : (w + 1) * boxes]

    def lower(i, slot, total):
        maps = jnp.concatenate([down[i * GROUP + w] for w in range(GROUP)], 1)
        return total + lax.dot_general(held[slot], maps, NT, preferred_element_type=F32)

    rows = rows_of(0)
    for w in range(GROUP):
        select(rows, 0, w)
    picked = jnp.dot(pick_ref[:, :half], near_ref[...], preferred_element_type=F32)
    picked += jnp.dot(pick_ref[:, half:], far_ref[...], preferred_element_type=F32)
    dens[...] = picked.astype(BF)
    ups[0].wait()
    equivalents(0, 0)

    due = {}
    for n, copy in enumerate(ups[1:]):
        first = GROUP if n == 0 else n * here
        due.setdefault(max(first // GROUP - 1, 0) // 2, []).append(copy)
    for n, copy in enumerate(downs):
        due.setdefault(n * here // GROUP // 2, []).append(copy)

    def step(b, total):
        for at, copies in due.items():

            @pl.when(b == at)
            def _():
                for copy in copies:
                    copy.wait()

        for h in (0, 1):
            now = b * 2 + h
            later = lax.rem(now + 1, steps)
            rows = rows_of(later)
            total = lower(jnp.maximum(now - 1, 0), 1 - h, total)
            for pair in range(GROUP // 2):
                gather(h, pair)
                select(rows, 1 - h, 2 * pair)
                select(rows, 1 - h, 2 * pair + 1)
            equivalents(later, 1 - h)
            translate(h)
        return total

    total = lax.fori_loop(0, steps // 2, step, jnp.zeros((boxes, p), F32))
    out_ref[...] = lower(steps - 1, 1, total).astype(BF)


def solution(mesh):
    x_chips, z_chips, cores = 4, 8, 2
    groups = [[(x * z_chips + z) * cores + c for x in range(x_chips) for z in range(z_chips)] for c in range(cores)]
    swap = [(i, i ^ 1) for i in range(x_chips * z_chips * cores)]

    def parts(densities, up_ops, trans_ops, down_ops, read_table, interaction):
        boxes, _, p = densities.shape
        wedges, c, _ = up_ops.shape
        wedge_here, length = interaction.shape[1:]
        wedge_groups = wedges // wedge_here
        slots = read_table.shape[1]
        chips = len(groups[0])
        half = chips * boxes
        width = length * boxes

        copies = jnp.broadcast_to(densities.reshape(1, boxes, p), (chips, boxes, p))
        near = lax.all_to_all(copies, "box", 0, 0, axis_index_groups=groups)
        near = near.reshape(half, p)

        lists = pl.pallas_call(
            pack_kernel,
            in_specs=[VMEM],
            out_specs=VMEM,
            out_shape=jax.ShapeDtypeStruct((wedge_here, width), BF),
            compiler_params=pltpu.CompilerParams(vmem_limit_bytes=4 << 20),
            name="pack",
        )(interaction.transpose(1, 2, 0))
        spread = [lists]
        for j in range(1, wedge_groups):
            spread.append(lax.ppermute(lists, "wedge", [(i, (i + j) % wedge_groups) for i in range(wedge_groups)]))
        place = jnp.stack([lax.axis_index("box") % cores, lax.axis_index("wedge")])

        pick, tcat = pl.pallas_call(
            table_kernel,
            in_specs=[SMEM, VMEM, VMEM],
            out_specs=[VMEM, VMEM],
            out_shape=[
                jax.ShapeDtypeStruct((slots, 2 * half), BF),
                jax.ShapeDtypeStruct((length * c, c), BF),
            ],
            compiler_params=pltpu.CompilerParams(vmem_limit_bytes=4 << 20),
            name="tables",
        )(place, read_table, trans_ops)

        far = lax.ppermute(near, "box", swap)

        out = pl.pallas_call(
            main_kernel,
            in_specs=[SMEM] + [VMEM] * (4 + wedge_groups) + [HBM, HBM],
            out_specs=VMEM,
            out_shape=jax.ShapeDtypeStruct((boxes, p), BF),
            scratch_shapes=[
                pltpu.VMEM((wedges, width), F32),
                pltpu.VMEM((slots, p), BF),
                pltpu.VMEM((2, GROUP // 2, 2 * slots, 2 * c), BF),
                pltpu.VMEM((2, GROUP // 2, width, 2 * slots), BF),
                pltpu.VMEM((2, GROUP * boxes, length * c), BF),
                pltpu.VMEM((2, boxes, GROUP * c), BF),
                pltpu.VMEM((wedges, c, p), BF),
                pltpu.VMEM((wedges, p, c), BF),
                pltpu.SemaphoreType.DMA((2, wedge_groups + 1)),
            ],
            compiler_params=pltpu.CompilerParams(vmem_limit_bytes=40 << 20),
            name="main",
        )(
            place, near, far, pick, tcat, *spread,
            pltpu.with_memory_space_constraint(up_ops, pltpu.HBM),
            pltpu.with_memory_space_constraint(down_ops, pltpu.HBM),
        )
        return out.reshape(boxes, 1, p)

    in_specs = (P("box", "wedge", None), P(), P(), P(), P("box", None), P("box", "wedge", None))
    out_specs = P("box", "wedge", None)
    return jax.shard_map(parts, mesh=mesh, in_specs=in_specs, out_specs=out_specs, check_vma=False)
```

time: 50.1 us -> 47.6 us (0.950)
  starting transfers between devices: 8.78 us -> 7.57 us
  waiting for transfers between devices: 1.53 us -> 0.83 us
  Pallas kernels: 14.8 us -> 14.2 us
    ppermute x3, starting transfers between devices: 5.06 us -> 3.85 us  [parts(): lax.ppermute(lists, 'wedge', [(i, (i + j) % wedge_groups) for i in range(...]
    ppermute x3, waiting for transfers between devices: 1.53 us -> 0.83 us  [parts(): lax.ppermute(lists, 'wedge', [(i, (i + j) % wedge_groups) for i in range(...]
    pallas_call x2, Pallas kernels: 14.5 us -> 13.9 us  [the longest x1 13.1 us: parts(): pl.pallas_call(main_kernel, in_specs=[SMEM] + [VMEM] * (4 + wedge_groups)...]
where the time goes in v3:
time: 47.6 us; the launch traced here: 47.3 us
  blocking collectives  21.3 us (45%)
  Pallas kernels  14.2 us (30%)
  starting transfers between devices  7.57 us (16%)
  local copies, waits for them, and re-layouts  3.35 us (7%)
  waiting for transfers between devices  0.83 us (2%)
    all_to_all x1, blocking collectives, parts(): near = lax.all_to_all(copies, 'box', 0, 0, axis_index_groups=groups)  21.3 us
    pallas_call x1, Pallas kernels, parts(): pl.pallas_call(main_kernel, in_specs=[SMEM] + [VMEM] * (4 + wedge_groups)...  13.1 us
    ppermute x3, starting transfers between devices, parts(): lax.ppermute(lists, 'wedge', [(i, (i + j) % wedge_groups) for i in range(...  3.85 us
    ppermute x1, starting transfers between devices, parts(): far = lax.ppermute(near, 'box', swap)  3.72 us
    unnamed x6, local copies, waits for them, and re-layouts  2.62 us
  transfers between devices with their start and end apart: 4, of which 2 were waited for; matrix products, arithmetic and copies ran while one was open for 0% of the time, Pallas kernels for 2%

profile of v3, /device:TPU:1, one launch (start us, length us, event | category | flops | bytes accessed | tf_op | source)
XLA Modules:
  0.0 47.3 jit_solution(13119359808019083943)
XLA Ops:
  0.0 0.7 %broadcast_in_dim.8 = bf16[32,32,128]{2,1,0:T(8,128)(2,1)S(1)} broadcast(bf16[32,128]{1,0:T(8,128)(2,1)} %bitcast.9), dimensions={1,2} | broadcast | bytes 270336 | tf_op jit(solution)/shard_map/broadcast_in_dim | solution.py:166
  0.7 21.3 %all_to_all.5 = bf16[32,32,128]{2,1,0:T(8,128)(2,1)S(1)} all-to-all(bf16[32,32,128]{2,1,0:T(8,128)(2,1)S(1)} %broadcast_in_dim.8), channel_id=1, replica_groups={{0,2,4,6,8,10,12,14,16,18,20,22,24,26,28,30,32,34,36,38,40,42,44,46,48,..., dimensions={0} | all-to-all | bytes 524288 | tf_op jit(solution)/shard_map/all_to_all | solution.py:167
  22.1 3.7 %collective-permute-start = (bf16[1024,128]{1,0:T(8,128)(2,1)S(1)}, bf16[1024,128]{1,0:T(8,128)(2,1)S(1)}, u32[]{:S(2)}, u32[]{:S(2)}) collective-permute-start(bf16[1024,128]{1,0:T(8,128)(2,1)S(1)} %bitcast.6), channel_id=1, source_target_pairs={{0,1},{1,0},{2,3},{3,2},{4,5},{5,4},{6,7},{7,6},{8,9},{9,8},{10,11... | collective-permute-start | bytes 786440 | tf_op jit(solution)/shard_map/ppermute | solution.py:195
  25.8 0.0 copy-start.1
  25.8 0.9 %copy-done.1 = s32[32,24,16]{0,2,1:T(8,128)S(1)} copy-done((s32[32,24,16]{0,2,1:T(8,128)S(1)}, s32[32,24,16]{0,2,1:T(8,128)}, u32[]{:S(2)}) %copy-start.1) | copy-done | bytes 49176
  26.7 0.3 pack.1.refs_0_
  27.0 2.8 %collective-permute-start.3 = (bf16[24,512]{1,0:T(8,128)(2,1)S(1)}, bf16[24,512]{1,0:T(8,128)(2,1)S(1)}, u32[]{:S(2)}, u32[]{:S(2)}) collective-permute-start(bf16[24,512]{1,0:T(8,128)(2,1)S(1)} %pack.1.refs_0_), channel_id=1, source_target_pairs={{0,192},{64,0},{128,64},{192,128},{1,193},{65,1},{129,65},{193,129... | collective-permute-start | bytes 73736 | tf_op jit(solution)/shard_map/ppermute | solution.py:180
  29.8 0.3 collective-permute-start.2
  30.1 0.7 %collective-permute-start.1 = (bf16[24,512]{1,0:T(8,128)(2,1)S(1)}, bf16[24,512]{1,0:T(8,128)(2,1)S(1)}, u32[]{:S(2)}, u32[]{:S(2)}) collective-permute-start(bf16[24,512]{1,0:T(8,128)(2,1)S(1)} %pack.1.refs_0_), channel_id=1, source_target_pairs={{0,64},{64,128},{128,192},{192,0},{1,65},{65,129},{129,193},{193,1... | collective-permute-start | bytes 73736 | tf_op jit(solution)/shard_map/ppermute | solution.py:180
  30.8 0.1 pad_add_fusion.place_ref
  30.9 0.0 copy-start
  30.9 1.0 %copy-done = bf16[16,128,128]{2,1,0:T(8,128)(2,1)S(1)} copy-done((bf16[16,128,128]{2,1,0:T(8,128)(2,1)S(1)}, bf16[16,128,128]{2,1,0:T(8,128)(2,1)}, u32[]{:S(2)}) %copy-start) | copy-done | bytes 524312
  31.9 0.0 copy-start.2
  31.9 0.7 %copy-done.2 = s32[1,128]{1,0:T(1,128)S(1)} copy-done((s32[1,128]{1,0:T(1,128)S(1)}, s32[1,128]{1,0:T(1,128)}, u32[]{:S(2)}) %copy-start.2) | copy-done | bytes 536
  32.6 0.8 %tables.1 = (bf16[128,2048]{1,0:T(8,128)(2,1)S(1)}, bf16[2048,128]{1,0:T(8,128)(2,1)S(1)}) custom-call(s32[2]{0:T(128)S(1)} %pad_add_fusion.place_ref, s32[1,128]{1,0:T(1,128)S(1)} %copy-done.2, bf16[16,128,128]{2,1,0:T(8,128)(2,1)S(1)} %copy-done), custom_call_target="tpu_custom_call" | custom-call | tf_op jit(solution)/shard_map/tables/pallas_call | solution.py:183
  33.4 0.0 collective-permute-done.3.refs_3_
  33.4 0.6 %collective-permute-done.2.refs_2_ = bf16[24,512]{1,0:T(8,128)(2,1)S(1)} collective-permute-done((bf16[24,512]{1,0:T(8,128)(2,1)S(1)}, bf16[24,512]{1,0:T(8,128)(2,1)S(1)}, u32[]{:S(2)}, u32[]{:S(2)}) %collective-permute-start.2) | collective-permute-done | bytes 24608 | tf_op jit(solution)/shard_map/ppermute | solution.py:180
  34.0 0.2 collective-permute-done.1.refs_1_
  34.2 0.0 collective-permute-done.far_ref
  34.2 13.1 %main.1 = bf16[32,128]{1,0:T(8,128)(2,1)} custom-call(s32[2]{0:T(128)S(1)} %pad_add_fusion.place_ref, bf16[1024,128]{1,0:T(8,128)(2,1)S(1)} %bitcast.7, bf16[1024,128]{1,0:T(8,128)(2,1)S(1)} %collective-permute-done.far_ref, bf16[128,2048]{1,0:T(8,128)(2,1)S(1)} %get-tuple-element.7.pick_ref, bf16[2048,128]{1,0:T(8,128)(2,1)S(1)} %get-tuple-element.8.tcat_ref, ...), custom_call_target="tpu_custom_call" | custom-call | tf_op jit(solution)/shard_map/main/pallas_call | solution.py:197
Async XLA Ops:
  22.1 12.2 %collective-permute-start = (bf16[1024,128]{1,0:T(8,128)(2,1)S(1)}, bf16[1024,128]{1,0:T(8,128)(2,1)S(1)}, u32[]{:S(2)}, u32[]{:S(2)}) collective-permute-start(bf16[1024,128]{1,0:T(8,128)(2,1)S(1)} %bitcast.6), channel_id=1, source_target_pairs={{0,1},{1,0},{2,3},{3,2},{4,5},{5,4},{6,7},{7,6},{8,9},{9,8},{10,11... | collective-permute-start | bytes 786440 | tf_op jit(solution)/shard_map/ppermute | solution.py:195
  25.8 0.9 %copy-start.1 = (s32[32,24,16]{0,2,1:T(8,128)S(1)}, s32[32,24,16]{0,2,1:T(8,128)}, u32[]{:S(2)}) copy-start(s32[32,24,16]{0,2,1:T(8,128)} %param.11) | copy-start | bytes 147460
  27.0 6.4 %collective-permute-start.3 = (bf16[24,512]{1,0:T(8,128)(2,1)S(1)}, bf16[24,512]{1,0:T(8,128)(2,1)S(1)}, u32[]{:S(2)}, u32[]{:S(2)}) collective-permute-start(bf16[24,512]{1,0:T(8,128)(2,1)S(1)} %pack.1.refs_0_), channel_id=1, source_target_pairs={{0,192},{64,0},{128,64},{192,128},{1,193},{65,1},{129,65},{193,129... | collective-permute-start | bytes 73736 | tf_op jit(solution)/shard_map/ppermute | solution.py:180
  29.8 4.2 %collective-permute-start.2 = (bf16[24,512]{1,0:T(8,128)(2,1)S(1)}, bf16[24,512]{1,0:T(8,128)(2,1)S(1)}, u32[]{:S(2)}, u32[]{:S(2)}) collective-permute-start(bf16[24,512]{1,0:T(8,128)(2,1)S(1)} %pack.1.refs_0_), channel_id=1, source_target_pairs={{0,128},{64,192},{128,0},{192,64},{1,129},{65,193},{129,1},{193,65... | collective-permute-start | bytes 73736 | tf_op jit(solution)/shard_map/ppermute | solution.py:180
  30.1 4.1 %collective-permute-start.1 = (bf16[24,512]{1,0:T(8,128)(2,1)S(1)}, bf16[24,512]{1,0:T(8,128)(2,1)S(1)}, u32[]{:S(2)}, u32[]{:S(2)}) collective-permute-start(bf16[24,512]{1,0:T(8,128)(2,1)S(1)} %pack.1.refs_0_), channel_id=1, source_target_pairs={{0,64},{64,128},{128,192},{192,0},{1,65},{65,129},{129,193},{193,1... | collective-permute-start | bytes 73736 | tf_op jit(solution)/shard_map/ppermute | solution.py:180
  30.9 1.0 %copy-start = (bf16[16,128,128]{2,1,0:T(8,128)(2,1)S(1)}, bf16[16,128,128]{2,1,0:T(8,128)(2,1)}, u32[]{:S(2)}) copy-start(bf16[16,128,128]{2,1,0:T(8,128)(2,1)} %trans_ref.1) | copy-start | bytes 1572868
  31.9 0.7 %copy-start.2 = (s32[1,128]{1,0:T(1,128)S(1)}, s32[1,128]{1,0:T(1,128)}, u32[]{:S(2)}) copy-start(s32[1,128]{1,0:T(1,128)} %table_ref.1) | copy-start | bytes 1540

commit v4 on v3

--- a/solution.py
+++ b/solution.py
@@ -64,10 +64,6 @@
 
     for n, ref in enumerate(list_refs):
         lists[n * here : (n + 1) * here, :] = ref[...].astype(F32)
-    blank = jnp.zeros((GROUP // 2, slots, c), BF)
-    for slot in range(2):
-        blocks[slot, :, :slots, c:] = blank
-        blocks[slot, :, slots:, :c] = blank
     held[1] = jnp.zeros(held.shape[1:], BF)
     number = lax.broadcasted_iota(jnp.int32, (slots, slots), 0).astype(F32)
     chunks = lists.shape[1] // slots
@@ -79,24 +75,18 @@
         for j in range(chunks):
             row = jnp.broadcast_to(rows[w : w + 1, j * slots : (j + 1) * slots], (slots, slots))
             hit = jnp.where(row == number, 1.0, 0.0).astype(BF)
-            sel[slot, w // 2, j * slots : (j + 1) * slots, w % 2 * slots : (w % 2 + 1) * slots] = hit.T
+            sel[slot, w, j * slots : (j + 1) * slots, :] = hit.T
 
     def equivalents(i, slot):
         maps = up[pl.ds(pl.multiple_of(i * GROUP, GROUP), GROUP)].reshape(GROUP * c, p)
         value = lax.dot_general(dens[...], maps, NT, preferred_element_type=F32).astype(BF)
         for w in range(GROUP):
-            blocks[slot, w // 2, w % 2 * slots : (w % 2 + 1) * slots, w % 2 * c : (w % 2 + 1) * c] = (
-                value[:, w * c : (w + 1) * c]
-            )
-
-    def gather(slot, pair):
-        sources = jnp.dot(sel[slot, pair], blocks[slot, pair], preferred_element_type=F32).astype(BF)
+            blocks[slot, w] = value[:, w * c : (w + 1) * c]
+
+    def gather(slot, w):
+        sources = jnp.dot(sel[slot, w], blocks[slot, w], preferred_element_type=F32).astype(BF)
         for k in range(length):
-            for d in range(2):
-                w = 2 * pair + d
-                wide[slot, w * boxes : (w + 1) * boxes, k * c : (k + 1) * c] = (
-                    sources[k * boxes : (k + 1) * boxes, d * c : (d + 1) * c]
-                )
+            wide[slot, w * boxes : (w + 1) * boxes, k * c : (k + 1) * c] = sources[k * boxes : (k + 1) * boxes]
 
     def translate(slot):
         local = jnp.dot(wide[slot], tcat_ref[...], preferred_element_type=F32).astype(BF)
@@ -136,10 +126,9 @@
             later = lax.rem(now + 1, steps)
             rows = rows_of(later)
             total = lower(jnp.maximum(now - 1, 0), 1 - h, total)
-            for pair in range(GROUP // 2):
-                gather(h, pair)
-                select(rows, 1 - h, 2 * pair)
-                select(rows, 1 - h, 2 * pair + 1)
+            for w in range(GROUP):
+                gather(h, w)
+                select(rows, 1 - h, w)
             equivalents(later, 1 - h)
             translate(h)
         return total
@@ -202,8 +191,8 @@
             scratch_shapes=[
                 pltpu.VMEM((wedges, width), F32),
                 pltpu.VMEM((slots, p), BF),
-                pltpu.VMEM((2, GROUP // 2, 2 * slots, 2 * c), BF),
-                pltpu.VMEM((2, GROUP // 2, width, 2 * slots), BF),
+                pltpu.VMEM((2, GROUP, slots, c), BF),
+                pltpu.VMEM((2, GROUP, width, slots), BF),
                 pltpu.VMEM((2, GROUP * boxes, length * c), BF),
                 pltpu.VMEM((2, boxes, GROUP * c), BF),
                 pltpu.VMEM((wedges, c, p), BF),

time: 47.6 us -> 47.2 us (level)
  Pallas kernels: 14.2 us -> 13.7 us
where the time goes in v4:
time: 47.2 us; the launch traced here: 46.9 us
  blocking collectives  21.3 us (45%)
  Pallas kernels  13.7 us (29%)
  starting transfers between devices  7.57 us (16%)
  local copies, waits for them, and re-layouts  3.35 us (7%)
  waiting for transfers between devices  0.83 us (2%)
    all_to_all x1, blocking collectives, parts(): near = lax.all_to_all(copies, 'box', 0, 0, axis_index_groups=groups)  21.3 us
    pallas_call x1, Pallas kernels, parts(): pl.pallas_call(main_kernel, in_specs=[SMEM] + [VMEM] * (4 + wedge_groups)...  12.7 us
    ppermute x3, starting transfers between devices, parts(): lax.ppermute(lists, 'wedge', [(i, (i + j) % wedge_groups) for i in range(...  3.85 us
    ppermute x1, starting transfers between devices, parts(): far = lax.ppermute(near, 'box', swap)  3.72 us
    unnamed x6, local copies, waits for them, and re-layouts  2.62 us
  transfers between devices with their start and end apart: 4, of which 2 were waited for; matrix products, arithmetic and copies ran while one was open for 0% of the time, Pallas kernels for 2%

profile of v4, /device:TPU:1, one launch (start us, length us, event | category | flops | bytes accessed | tf_op | source)
XLA Modules:
  0.0 46.9 jit_solution(8840894764077104681)
XLA Ops:
  0.0 0.7 %broadcast_in_dim.8 = bf16[32,32,128]{2,1,0:T(8,128)(2,1)S(1)} broadcast(bf16[32,128]{1,0:T(8,128)(2,1)} %bitcast.9), dimensions={1,2} | broadcast | bytes 270336 | tf_op jit(solution)/shard_map/broadcast_in_dim | solution.py:155
  0.7 21.3 %all_to_all.5 = bf16[32,32,128]{2,1,0:T(8,128)(2,1)S(1)} all-to-all(bf16[32,32,128]{2,1,0:T(8,128)(2,1)S(1)} %broadcast_in_dim.8), channel_id=1, replica_groups={{0,2,4,6,8,10,12,14,16,18,20,22,24,26,28,30,32,34,36,38,40,42,44,46,48,..., dimensions={0} | all-to-all | bytes 524288 | tf_op jit(solution)/shard_map/all_to_all | solution.py:156
  22.1 3.7 %collective-permute-start = (bf16[1024,128]{1,0:T(8,128)(2,1)S(1)}, bf16[1024,128]{1,0:T(8,128)(2,1)S(1)}, u32[]{:S(2)}, u32[]{:S(2)}) collective-permute-start(bf16[1024,128]{1,0:T(8,128)(2,1)S(1)} %bitcast.6), channel_id=1, source_target_pairs={{0,1},{1,0},{2,3},{3,2},{4,5},{5,4},{6,7},{7,6},{8,9},{9,8},{10,11... | collective-permute-start | bytes 786440 | tf_op jit(solution)/shard_map/ppermute | solution.py:184
  25.8 0.0 copy-start.1
  25.8 0.9 %copy-done.1 = s32[32,24,16]{0,2,1:T(8,128)S(1)} copy-done((s32[32,24,16]{0,2,1:T(8,128)S(1)}, s32[32,24,16]{0,2,1:T(8,128)}, u32[]{:S(2)}) %copy-start.1) | copy-done | bytes 49176
  26.7 0.3 pack.1.refs_0_
  27.0 2.8 %collective-permute-start.3 = (bf16[24,512]{1,0:T(8,128)(2,1)S(1)}, bf16[24,512]{1,0:T(8,128)(2,1)S(1)}, u32[]{:S(2)}, u32[]{:S(2)}) collective-permute-start(bf16[24,512]{1,0:T(8,128)(2,1)S(1)} %pack.1.refs_0_), channel_id=1, source_target_pairs={{0,192},{64,0},{128,64},{192,128},{1,193},{65,1},{129,65},{193,129... | collective-permute-start | bytes 73736 | tf_op jit(solution)/shard_map/ppermute | solution.py:169
  29.8 0.3 collective-permute-start.2
  30.1 0.7 %collective-permute-start.1 = (bf16[24,512]{1,0:T(8,128)(2,1)S(1)}, bf16[24,512]{1,0:T(8,128)(2,1)S(1)}, u32[]{:S(2)}, u32[]{:S(2)}) collective-permute-start(bf16[24,512]{1,0:T(8,128)(2,1)S(1)} %pack.1.refs_0_), channel_id=1, source_target_pairs={{0,64},{64,128},{128,192},{192,0},{1,65},{65,129},{129,193},{193,1... | collective-permute-start | bytes 73736 | tf_op jit(solution)/shard_map/ppermute | solution.py:169
  30.8 0.1 pad_add_fusion.place_ref
  30.9 0.0 copy-start
  30.9 1.0 %copy-done = bf16[16,128,128]{2,1,0:T(8,128)(2,1)S(1)} copy-done((bf16[16,128,128]{2,1,0:T(8,128)(2,1)S(1)}, bf16[16,128,128]{2,1,0:T(8,128)(2,1)}, u32[]{:S(2)}) %copy-start) | copy-done | bytes 524312
  31.9 0.0 copy-start.2
  31.9 0.7 %copy-done.2 = s32[1,128]{1,0:T(1,128)S(1)} copy-done((s32[1,128]{1,0:T(1,128)S(1)}, s32[1,128]{1,0:T(1,128)}, u32[]{:S(2)}) %copy-start.2) | copy-done | bytes 536
  32.6 0.8 %tables.1 = (bf16[128,2048]{1,0:T(8,128)(2,1)S(1)}, bf16[2048,128]{1,0:T(8,128)(2,1)S(1)}) custom-call(s32[2]{0:T(128)S(1)} %pad_add_fusion.place_ref, s32[1,128]{1,0:T(1,128)S(1)} %copy-done.2, bf16[16,128,128]{2,1,0:T(8,128)(2,1)S(1)} %copy-done), custom_call_target="tpu_custom_call" | custom-call | tf_op jit(solution)/shard_map/tables/pallas_call | solution.py:172
  33.4 0.0 collective-permute-done.3.refs_3_
  33.4 0.6 %collective-permute-done.2.refs_2_ = bf16[24,512]{1,0:T(8,128)(2,1)S(1)} collective-permute-done((bf16[24,512]{1,0:T(8,128)(2,1)S(1)}, bf16[24,512]{1,0:T(8,128)(2,1)S(1)}, u32[]{:S(2)}, u32[]{:S(2)}) %collective-permute-start.2) | collective-permute-done | bytes 24608 | tf_op jit(solution)/shard_map/ppermute | solution.py:169
  34.0 0.2 collective-permute-done.1.refs_1_
  34.2 0.0 collective-permute-done.far_ref
  34.2 12.7 %main.1 = bf16[32,128]{1,0:T(8,128)(2,1)} custom-call(s32[2]{0:T(128)S(1)} %pad_add_fusion.place_ref, bf16[1024,128]{1,0:T(8,128)(2,1)S(1)} %bitcast.7, bf16[1024,128]{1,0:T(8,128)(2,1)S(1)} %collective-permute-done.far_ref, bf16[128,2048]{1,0:T(8,128)(2,1)S(1)} %get-tuple-element.7.pick_ref, bf16[2048,128]{1,0:T(8,128)(2,1)S(1)} %get-tuple-element.8.tcat_ref, ...), custom_call_target="tpu_custom_call" | custom-call | tf_op jit(solution)/shard_map/main/pallas_call | solution.py:186
Async XLA Ops:
  22.1 12.2 %collective-permute-start = (bf16[1024,128]{1,0:T(8,128)(2,1)S(1)}, bf16[1024,128]{1,0:T(8,128)(2,1)S(1)}, u32[]{:S(2)}, u32[]{:S(2)}) collective-permute-start(bf16[1024,128]{1,0:T(8,128)(2,1)S(1)} %bitcast.6), channel_id=1, source_target_pairs={{0,1},{1,0},{2,3},{3,2},{4,5},{5,4},{6,7},{7,6},{8,9},{9,8},{10,11... | collective-permute-start | bytes 786440 | tf_op jit(solution)/shard_map/ppermute | solution.py:184
  25.8 0.9 %copy-start.1 = (s32[32,24,16]{0,2,1:T(8,128)S(1)}, s32[32,24,16]{0,2,1:T(8,128)}, u32[]{:S(2)}) copy-start(s32[32,24,16]{0,2,1:T(8,128)} %param.11) | copy-start | bytes 147460
  27.0 6.4 %collective-permute-start.3 = (bf16[24,512]{1,0:T(8,128)(2,1)S(1)}, bf16[24,512]{1,0:T(8,128)(2,1)S(1)}, u32[]{:S(2)}, u32[]{:S(2)}) collective-permute-start(bf16[24,512]{1,0:T(8,128)(2,1)S(1)} %pack.1.refs_0_), channel_id=1, source_target_pairs={{0,192},{64,0},{128,64},{192,128},{1,193},{65,1},{129,65},{193,129... | collective-permute-start | bytes 73736 | tf_op jit(solution)/shard_map/ppermute | solution.py:169
  29.8 4.2 %collective-permute-start.2 = (bf16[24,512]{1,0:T(8,128)(2,1)S(1)}, bf16[24,512]{1,0:T(8,128)(2,1)S(1)}, u32[]{:S(2)}, u32[]{:S(2)}) collective-permute-start(bf16[24,512]{1,0:T(8,128)(2,1)S(1)} %pack.1.refs_0_), channel_id=1, source_target_pairs={{0,128},{64,192},{128,0},{192,64},{1,129},{65,193},{129,1},{193,65... | collective-permute-start | bytes 73736 | tf_op jit(solution)/shard_map/ppermute | solution.py:169
  30.1 4.1 %collective-permute-start.1 = (bf16[24,512]{1,0:T(8,128)(2,1)S(1)}, bf16[24,512]{1,0:T(8,128)(2,1)S(1)}, u32[]{:S(2)}, u32[]{:S(2)}) collective-permute-start(bf16[24,512]{1,0:T(8,128)(2,1)S(1)} %pack.1.refs_0_), channel_id=1, source_target_pairs={{0,64},{64,128},{128,192},{192,0},{1,65},{65,129},{129,193},{193,1... | collective-permute-start | bytes 73736 | tf_op jit(solution)/shard_map/ppermute | solution.py:169
  30.9 1.0 %copy-start = (bf16[16,128,128]{2,1,0:T(8,128)(2,1)S(1)}, bf16[16,128,128]{2,1,0:T(8,128)(2,1)}, u32[]{:S(2)}) copy-start(bf16[16,128,128]{2,1,0:T(8,128)(2,1)} %trans_ref.1) | copy-start | bytes 1572868
  31.9 0.7 %copy-start.2 = (s32[1,128]{1,0:T(1,128)S(1)}, s32[1,128]{1,0:T(1,128)}, u32[]{:S(2)}) copy-start(s32[1,128]{1,0:T(1,128)} %table_ref.1) | copy-start | bytes 1540
